TPU v7x, 32 devices: a whole 2x2x4 slice. The times are simulated.
32 devices in a mesh: dp: 4 (over x, core), expert: 8 (over z, y).
Axes of the slice: x: 2, y: 2, z: 4, core: 2. Of those that a mesh axis runs over, the one named last changes fastest.
Arguments:
- tokens: bfloat16 [4096, 2048], P(('dp', 'expert')), may hold values from -6 to 6
- cotangent: bfloat16 [4096, 2048], P(('dp', 'expert')), may hold values from -1.5 to 1.5
- gate_score: bfloat16 [4096], P(('dp', 'expert')), may hold values from 0.19921875 to 1
- block_expert: int32 [256], P(('dp', 'expert')), may hold values from 0 to 7, as said below
- expert_slot: int32 [8], replicated, may hold values from 0 to 7, each once
- up_weight: bfloat16 [8, 2048, 704], P('expert'), may hold values from -0.125 to 0.125
- down_weight: bfloat16 [8, 2048, 704], P('expert'), may hold values from -0.21875 to 0.21875
Outputs:
- token_grad: bfloat16 [4096, 2048], P(('dp', 'expert'))
- gate_grad: bfloat16 [4096], P(('dp', 'expert'))
- grad_up: bfloat16 [8, 2048, 704], P('expert', 'dp')
- grad_down: bfloat16 [8, 2048, 704], P('expert', 'dp')
Inputs may be any that keep to these rules, and one draw needn't show every extreme that they name: `block_expert`: the 8 blocks of each device name every expert exactly once. `expert_slot`: each slot holds exactly one expert.
All inputs are finite; a program needn't handle non-finite values.
Results may differ from a plain program's by a relative error of at most 0.0085.
Values may be sent and summed in bfloat16 or wider, within the bound.
A program may use at most 64 MiB of HBM per device.

v0:
```python
import jax
import jax.numpy as jnp
from jax import lax
from jax.sharding import PartitionSpec as P


def silu_slope(pre_act):
    logistic = jax.nn.sigmoid(pre_act)
    return logistic * (1.0 + pre_act * (1.0 - logistic))


def arrange(values, order_index, peer_count):
    shaped = values.reshape((peer_count, values.shape[0] // peer_count) + values.shape[1:])
    return jnp.take(shaped, order_index, axis=0).reshape(values.shape)


def local(tokens, cotangent, gate_score, block_expert, expert_slot, up_weight, down_weight):
    row_count, model_width = tokens.shape
    hidden_width = up_weight.shape[2]
    peer_count = lax.axis_size("expert")
    share_rows = model_width // lax.axis_size("dp")
    expert_count = expert_slot.shape[0]
    chosen = (block_expert[:, None] == jnp.arange(expert_count, dtype=jnp.int32)[None, :]).astype(
        jnp.int32
    )
    block_slot = jnp.sum(chosen * expert_slot[None, :], axis=1)
    places = jnp.arange(peer_count, dtype=jnp.int32)
    matches = (block_slot[None, :] == places[:, None]).astype(jnp.int32)
    source = jnp.sum(matches * places[None, :], axis=1)
    outbound = (
        arrange(tokens, source, peer_count),
        arrange(cotangent, source, peer_count),
        arrange(gate_score, source, peer_count),
    )
    inputs, upstream, gate_rows = (
        lax.all_to_all(outbound[0], "expert", split_axis=0, concat_axis=0, tiled=True),
        lax.all_to_all(outbound[1], "expert", split_axis=0, concat_axis=0, tiled=True),
        lax.all_to_all(outbound[2], "expert", split_axis=0, concat_axis=0, tiled=True),
    )
    up_mat = up_weight[0]
    down_mat = down_weight[0]
    contract_last = (((1,), (1,)), ((), ()))
    pre_act = jnp.dot(inputs, up_mat, preferred_element_type=jnp.float32)
    hidden = jax.nn.silu(pre_act).astype(jnp.bfloat16)
    expert_out = lax.dot_general(
        hidden, down_mat, contract_last, preferred_element_type=jnp.float32
    )
    gate_grad = jnp.sum(upstream.astype(jnp.float32) * expert_out, axis=1).astype(jnp.bfloat16)
    scaled = (gate_rows.astype(jnp.float32)[:, None] * upstream.astype(jnp.float32)).astype(
        jnp.bfloat16
    )
    hidden_grad = jnp.dot(scaled, down_mat, preferred_element_type=jnp.float32)
    pre_grad = (hidden_grad * silu_slope(pre_act)).astype(jnp.bfloat16)
    input_grad = lax.dot_general(
        pre_grad, up_mat, contract_last, preferred_element_type=jnp.float32
    ).astype(jnp.bfloat16)
    returned, gate_back = (
        lax.all_to_all(input_grad, "expert", split_axis=0, concat_axis=0, tiled=True),
        lax.all_to_all(gate_grad, "expert", split_axis=0, concat_axis=0, tiled=True),
    )
    columns = (
        lax.all_to_all(inputs, "dp", split_axis=1, concat_axis=0, tiled=True),
        lax.all_to_all(scaled, "dp", split_axis=1, concat_axis=0, tiled=True),
    )
    pieces = (
        lax.all_gather(pre_grad, "dp", axis=0, tiled=True),
        lax.all_gather(hidden, "dp", axis=0, tiled=True),
    )
    row_total = pieces[0].shape[0]
    shards = row_total // row_count
    input_rows = columns[0].reshape(shards, row_count, share_rows)
    scaled_rows = columns[1].reshape(shards, row_count, share_rows)
    grad_rows = pieces[0].reshape(shards, row_count, hidden_width)
    hidden_rows = pieces[1].reshape(shards, row_count, hidden_width)
    up_partial = jnp.einsum(
        "krc,krh->kch", input_rows, grad_rows, preferred_element_type=jnp.float32
    ).astype(jnp.bfloat16)
    down_partial = jnp.einsum(
        "krc,krh->kch", scaled_rows, hidden_rows, preferred_element_type=jnp.float32
    ).astype(jnp.bfloat16)
    grad_up = jnp.sum(up_partial.astype(jnp.float32), axis=0)
    grad_down = jnp.sum(down_partial.astype(jnp.float32), axis=0)
    token_grad = arrange(returned, block_slot, peer_count)
    gate_out = arrange(gate_back, block_slot, peer_count)
    return (
        token_grad,
        gate_out,
        grad_up.astype(jnp.bfloat16)[None],
        grad_down.astype(jnp.bfloat16)[None],
    )


def solution(mesh):
    return jax.shard_map(
        local,
        mesh=mesh,
        in_specs=(
            P(("dp", "expert"), None),
            P(("dp", "expert"), None),
            P(("dp", "expert")),
            P(("dp", "expert")),
            P(),
            P("expert", None, None),
            P("expert", None, None),
        ),
        out_specs=(
            P(("dp", "expert"), None),
            P(("dp", "expert")),
            P("expert", "dp", None),
            P("expert", "dp", None),
        ),
        check_vma=False,
    )
```

profile of v0, /device:TPU:0, one launch (start us, length us, event | category | flops | bytes accessed | tf_op | source)
XLA Modules:
  0.0 127.9 jit_solution(4773708059999306015)
XLA Ops:
  0.6 0.0 copy-start
  0.6 1.0 select_reduce_fusion.1
  1.7 0.1 select_reduce_fusion
  1.8 0.7 reshape.112
  2.5 0.6 gather_fusion
  3.1 0.1 select_bitcast_fusion
  3.2 0.6 copy.31
  3.8 7.3 %all-to-all-start = ((bf16[8,16,1]{1,2,0:T(2,128)(2,1)}), bf16[8,16,1]{1,2,0:T(2,128)(2,1)S(1)}, u32[]{:S(2)}, u32[]{:S(2)}) async-start(bf16[8,16,1]{1,2,0:T(2,128)(2,1)} %copy.31), calls=%async_computation | async-start | bytes 8192 | tf_op jit(solution)/shard_map/all_to_all | solution.py:38
  11.1 2.4 %gather_fusion.2 = bf16[8,16,2048]{2,1,0:T(8,128)(2,1)} fusion(bf16[8,16,2048]{2,1,0:T(8,128)(2,1)} %bitcast.67, s32[1024]{0:T(1024)S(1)} %pad_clamp_fusion.1), kind=kCustom, calls=%fused_computation.3.clone | custom fusion | bytes 1048608 | tf_op jit(solution)/shard_map/jit(_take)/gather | solution.py:14
  13.5 2.4 %gather_fusion.1 = bf16[8,16,2048]{2,1,0:T(8,128)(2,1)} fusion(bf16[8,16,2048]{2,1,0:T(8,128)(2,1)} %bitcast.68, s32[1024]{0:T(1024)S(1)} %pad_clamp_fusion.1), kind=kCustom, calls=%fused_computation.1.clone | custom fusion | bytes 1048608 | tf_op jit(solution)/shard_map/jit(_take)/gather | solution.py:14
  15.9 2.2 %broadcast_select_fusion.1 = (bf16[8,16,2048]{2,1,0:T(8,128)(2,1)S(1)}, bf16[8,16,2048]{2,1,0:T(8,128)(2,1)}) fusion(bf16[8,16,2048]{2,1,0:T(8,128)(2,1)} %gather_fusion.2, pred[8]{0:T(512)(128)(4,1)S(1)} %compare_and_fusion.1, bf16[8,16,2048]{2,1,0:T(8,128)(2,1)} %gather_fusion.1), kind=kLoop, calls=%fused_computation.30 | loop fusion | flops 524288 | bytes 2097160 | tf_op jit(solution)/shard_map/jit(_take)/select_n | solution.py:14
  18.0 0.0 all-to-all-done
  18.0 19.8 %all_to_all.68 = bf16[8,16,2048]{2,1,0:T(8,128)(2,1)} all-to-all(bf16[8,16,2048]{2,1,0:T(8,128)(2,1)S(1)} %get-tuple-element.8), channel_id=1, replica_groups=mesh['dp'=4,'expert'=8] {'expert'}, dimensions={0} | all-to-all | bytes 1048576 | tf_op jit(solution)/shard_map/all_to_all | solution.py:36
  37.9 3.6 %all-to-all-start.1 = ((bf16[8,16,2048]{2,1,0:T(8,128)(2,1)}), bf16[8,16,2048]{2,1,0:T(8,128)(2,1)S(1)}, u32[]{:S(2)}, u32[]{:S(2)}) async-start(bf16[8,16,2048]{2,1,0:T(8,128)(2,1)} %get-tuple-element.9), calls=%async_computation.1 | async-start | bytes 1048576 | tf_op jit(solution)/shard_map/all_to_all | solution.py:37
  41.5 0.1 reshape.122
  41.6 0.0 copy-done
  41.6 2.8 %multiply_convert_fusion.1 = (bf16[128,704]{0,1:T(8,128)(2,1)}, f32[128,704]{0,1:T(8,128)}) fusion(bf16[128,2048]{1,0:T(8,128)(2,1)} %bitcast.65, bf16[1,2048,704]{1,2,0:T(8,128)(2,1)S(1)} %copy-done), kind=kOutput, calls=%fused_computation.32 | convolution fusion | flops 369549312 | bytes 3948544 | tf_op jit(solution)/shard_map/dot_general | solution.py:43
  44.4 11.1 %all-to-all-done.1 = bf16[8,16,2048]{2,1,0:T(8,128)(2,1)S(1)} async-done(((bf16[8,16,2048]{2,1,0:T(8,128)(2,1)}), bf16[8,16,2048]{2,1,0:T(8,128)(2,1)S(1)}, u32[]{:S(2)}, u32[]{:S(2)}) %all-to-all-start.1) | async-done | bytes 524320 | tf_op jit(solution)/shard_map/all_to_all | solution.py:37
  55.5 0.1 convert_element_type.77
  55.6 2.6 %fusion.14 = bf16[128]{0:T(256)(128)(2,1)S(1)} fusion(f32[128,2048]{1,0:T(8,128)S(1)} %bitcast.64, bf16[128,704]{0,1:T(8,128)(2,1)} %get-tuple-element.10, bf16[1,2048,704]{1,2,0:T(8,128)(2,1)} %param.17), kind=kOutput, calls=%fused_computation.17 | convolution fusion | flops 369622912 | bytes 4112640 | tf_op jit(solution)/shard_map/dot_general | solution.py:45
  58.3 0.7 convert_element_type.98
  58.9 3.6 %all-to-all-start.4 = ((bf16[8,16,1]{1,2,0:T(2,128)(2,1)}), bf16[8,16,1]{1,2,0:T(2,128)(2,1)S(1)}, u32[]{:S(2)}, u32[]{:S(2)}) async-start(bf16[8,16,1]{1,2,0:T(2,128)(2,1)} %convert_element_type.98), calls=%async_computation.4 | async-start | bytes 8192 | tf_op jit(solution)/shard_map/all_to_all | solution.py:59
  62.6 0.9 multiply_convert_fusion
  63.5 2.2 %all_to_all.56 = bf16[128,4,512]{2,1,0:T(4,128)(2,1)} reshape(bf16[8,16,2048]{2,1,0:T(8,128)(2,1)} %all_to_all.68) | data formatting | bytes 1048576 | tf_op jit(solution)/shard_map/all_to_all | solution.py:62
  65.8 1.9 %copy.34 = bf16[128,4,512]{2,0,1:T(8,128)(2,1)} copy(bf16[128,4,512]{2,1,0:T(4,128)(2,1)} %all_to_all.56) | data formatting | bytes 1048576 | tf_op jit(solution)/shard_map/all_to_all | solution.py:62
  67.7 1.7 %reshape.123 = f32[128,4,512]{2,1,0:T(4,128)} reshape(bf16[8,16,2048]{2,1,0:T(8,128)(2,1)S(1)} %all-to-all-done.1) | data formatting | bytes 1572864 | tf_op jit(solution)/shard_map/convert_element_type | solution.py:49
  69.4 0.0 all-to-all-done.4
  69.4 4.1 %all-to-all-start.5 = ((bf16[128,4,512]{2,0,1:T(8,128)(2,1)}), bf16[128,4,512]{2,0,1:T(8,128)(2,1)}, u32[]{:S(2)}, u32[]{:S(2)}) async-start(bf16[128,4,512]{2,0,1:T(8,128)(2,1)} %copy.34), calls=%async_computation.5 | async-start | bytes 1048576 | tf_op jit(solution)/shard_map/all_to_all | solution.py:62
  73.6 2.3 %fusion.23 = bf16[128,4,512]{2,0,1:T(8,128)(2,1)} fusion(f32[128,4,512]{2,1,0:T(4,128)} %reshape.123, f32[128]{0:T(128)S(1)} %reshape.122), kind=kLoop, calls=%fused_computation.21 | loop fusion | flops 524288 | bytes 1573376 | tf_op jit(solution)/shard_map/convert_element_type | solution.py:49
  75.9 2.9 %fusion.20 = bf16[128,704]{0,1:T(8,128)(2,1)S(1)} fusion(bf16[128,2048]{1,0:T(8,128)(2,1)} %bitcast.66, bf16[1,2048,704]{1,2,0:T(8,128)(2,1)} %param.17, f32[128,704]{0,1:T(8,128)} %get-tuple-element.11), kind=kOutput, calls=%fused_computation.19 | convolution fusion | flops 369909760 | bytes 3948544 | tf_op jit(solution)/shard_map/dot_general | solution.py:52
  78.8 3.6 %all-to-all-done.5 = bf16[128,4,512]{2,0,1:T(8,128)(2,1)} async-done(((bf16[128,4,512]{2,0,1:T(8,128)(2,1)}), bf16[128,4,512]{2,0,1:T(8,128)(2,1)}, u32[]{:S(2)}, u32[]{:S(2)}) %all-to-all-start.5) | async-done | bytes 524320 | tf_op jit(solution)/shard_map/all_to_all | solution.py:62
  82.5 4.1 %all-to-all-start.6 = ((bf16[128,4,512]{2,0,1:T(8,128)(2,1)}), bf16[128,4,512]{2,0,1:T(8,128)(2,1)}, u32[]{:S(2)}, u32[]{:S(2)}) async-start(bf16[128,4,512]{2,0,1:T(8,128)(2,1)} %fusion.23), calls=%async_computation.6 | async-start | bytes 1048576 | tf_op jit(solution)/shard_map/all_to_all | solution.py:63
  86.6 14.0 %all_gather.6 = bf16[512,704]{0,1:T(8,128)(2,1)} all-gather(bf16[128,704]{0,1:T(8,128)(2,1)S(1)} %fusion.20), channel_id=1, replica_groups=mesh['dp'=4,'expert'=8] {'dp'}, dimensions={0}, use_global_device_ids=true | all-gather | bytes 901120 | tf_op jit(solution)/shard_map/all_gather | solution.py:66
  100.6 1.4 %fusion.11 = bf16[128,2048]{1,0:T(8,128)(2,1)} fusion(bf16[128,704]{0,1:T(8,128)(2,1)S(1)} %fusion.20, bf16[1,2048,704]{1,2,0:T(8,128)(2,1)S(1)} %copy-done), kind=kOutput, calls=%fused_computation.16 | convolution fusion | flops 369360896 | bytes 3588096 | tf_op jit(solution)/shard_map/dot_general | solution.py:54
  102.0 0.0 all-to-all-done.6
  102.0 6.0 %all-to-all-start.3 = ((bf16[8,16,2048]{2,1,0:T(8,128)(2,1)}), bf16[8,16,2048]{2,1,0:T(8,128)(2,1)S(1)}, u32[]{:S(2)}, u32[]{:S(2)}) async-start(bf16[8,16,2048]{2,1,0:T(8,128)(2,1)} %bitcast.8), calls=%async_computation.3 | async-start | bytes 1048576 | tf_op jit(solution)/shard_map/all_to_all | solution.py:58
  108.0 8.9 %all_gather.7 = bf16[512,704]{0,1:T(8,128)(2,1)} all-gather(bf16[128,704]{0,1:T(8,128)(2,1)} %get-tuple-element.10), channel_id=1, replica_groups=mesh['dp'=4,'expert'=8] {'dp'}, dimensions={0}, use_global_device_ids=true | all-gather | bytes 901120 | tf_op jit(solution)/shard_map/all_gather | solution.py:67
  117.0 0.6 gather_fusion.4
  117.5 0.1 broadcast_select_fusion.3
  117.6 0.6 reshape.117
  118.2 3.2 %convert_reduce_fusion.1 = bf16[512,704]{0,1:T(8,128)(2,1)} fusion(bf16[128,4,512]{2,0,1:T(8,128)(2,1)} %all-to-all-done.5, bf16[512,704]{0,1:T(8,128)(2,1)} %all_gather.6), kind=kOutput, calls=%fused_computation.14 | convolution fusion | flops 371621888 | bytes 1966080 | tf_op jit(solution)/shard_map/krc,krh->kch/dot_general | solution.py:75
  121.4 3.2 %convert_reduce_fusion = bf16[512,704]{0,1:T(8,128)(2,1)} fusion(bf16[128,4,512]{2,0,1:T(8,128)(2,1)} %all-to-all-done.6, bf16[512,704]{0,1:T(8,128)(2,1)} %all_gather.7), kind=kOutput, calls=%fused_computation.13 | convolution fusion | flops 371621888 | bytes 1966080 | tf_op jit(solution)/shard_map/krc,krh->kch/dot_general | solution.py:78
  124.5 0.0 all-to-all-done.3
  124.5 1.4 %gather_fusion.3 = bf16[8,16,2048]{2,1,0:T(8,128)(2,1)} fusion(bf16[8,16,2048]{2,1,0:T(8,128)(2,1)S(1)} %all-to-all-done.3, s32[1024]{0:T(1024)S(1)} %pad_clamp_fusion), kind=kCustom, calls=%fused_computation.4.clone | custom fusion | bytes 1048608 | tf_op jit(solution)/shard_map/jit(_take)/gather | solution.py:14
  125.9 1.9 %broadcast_select_fusion = bf16[8,16,2048]{2,1,0:T(8,128)(2,1)} fusion(bf16[8,16,2048]{2,1,0:T(8,128)(2,1)} %gather_fusion.3, pred[8]{0:T(512)(128)(4,1)S(1)} %compare_and_fusion), kind=kLoop, calls=%fused_computation.29 | loop fusion | flops 262144 | bytes 1048584 | tf_op jit(solution)/shard_map/jit(_take)/select_n | solution.py:14
  (8 shorter events, 0.0 us)
Async XLA Ops:
  0.6 41.0 %copy-start = (bf16[1,2048,704]{1,2,0:T(8,128)(2,1)S(1)}, bf16[1,2048,704]{1,2,0:T(8,128)(2,1)}, u32[]{:S(2)}) copy-start(bf16[1,2048,704]{1,2,0:T(8,128)(2,1)} %param.16) | copy-start | bytes 8650756
  3.8 14.3 %all-to-all-start = ((bf16[8,16,1]{1,2,0:T(2,128)(2,1)}), bf16[8,16,1]{1,2,0:T(2,128)(2,1)S(1)}, u32[]{:S(2)}, u32[]{:S(2)}) async-start(bf16[8,16,1]{1,2,0:T(2,128)(2,1)} %copy.31), calls=%async_computation | async-start | bytes 8192 | tf_op jit(solution)/shard_map/all_to_all | solution.py:38
  37.9 17.7 %all-to-all-start.1 = ((bf16[8,16,2048]{2,1,0:T(8,128)(2,1)}), bf16[8,16,2048]{2,1,0:T(8,128)(2,1)S(1)}, u32[]{:S(2)}, u32[]{:S(2)}) async-start(bf16[8,16,2048]{2,1,0:T(8,128)(2,1)} %get-tuple-element.9), calls=%async_computation.1 | async-start | bytes 1048576 | tf_op jit(solution)/shard_map/all_to_all | solution.py:37
  58.9 10.5 %all-to-all-start.4 = ((bf16[8,16,1]{1,2,0:T(2,128)(2,1)}), bf16[8,16,1]{1,2,0:T(2,128)(2,1)S(1)}, u32[]{:S(2)}, u32[]{:S(2)}) async-start(bf16[8,16,1]{1,2,0:T(2,128)(2,1)} %convert_element_type.98), calls=%async_computation.4 | async-start | bytes 8192 | tf_op jit(solution)/shard_map/all_to_all | solution.py:59
  69.4 13.1 %all-to-all-start.5 = ((bf16[128,4,512]{2,0,1:T(8,128)(2,1)}), bf16[128,4,512]{2,0,1:T(8,128)(2,1)}, u32[]{:S(2)}, u32[]{:S(2)}) async-start(bf16[128,4,512]{2,0,1:T(8,128)(2,1)} %copy.34), calls=%async_computation.5 | async-start | bytes 1048576 | tf_op jit(solution)/shard_map/all_to_all | solution.py:62
  82.5 19.5 %all-to-all-start.6 = ((bf16[128,4,512]{2,0,1:T(8,128)(2,1)}), bf16[128,4,512]{2,0,1:T(8,128)(2,1)}, u32[]{:S(2)}, u32[]{:S(2)}) async-start(bf16[128,4,512]{2,0,1:T(8,128)(2,1)} %fusion.23), calls=%async_computation.6 | async-start | bytes 1048576 | tf_op jit(solution)/shard_map/all_to_all | solution.py:63
  102.0 22.5 %all-to-all-start.3 = ((bf16[8,16,2048]{2,1,0:T(8,128)(2,1)}), bf16[8,16,2048]{2,1,0:T(8,128)(2,1)S(1)}, u32[]{:S(2)}, u32[]{:S(2)}) async-start(bf16[8,16,2048]{2,1,0:T(8,128)(2,1)} %bitcast.8), calls=%async_computation.3 | async-start | bytes 1048576 | tf_op jit(solution)/shard_map/all_to_all | solution.py:58
where the time goes:
time: 129 us; the launch traced here: 128 us
  blocking collectives  42.8 us (33%)
  starting transfers between devices  28.8 us (22%)
  matrix products  16 us (12%)
  local copies, waits for them, and re-layouts  15.9 us (12%)
  waiting for transfers between devices  14.8 us (11%)
  other arithmetic  8.8 us (7%)
    all_to_all x1, blocking collectives, local(): lax.all_to_all(outbound[0], 'expert', split_axis=0, concat_axis=0, tiled=...  19.8 us
    all_gather x1, blocking collectives, local(): lax.all_gather(pre_grad, 'dp', axis=0, tiled=True)  14 us
    all_to_all x1, waiting for transfers between devices, local(): lax.all_to_all(outbound[1], 'expert', split_axis=0, concat_axis=0, tiled=...  11.1 us
    all_gather x1, blocking collectives, local(): lax.all_gather(hidden, 'dp', axis=0, tiled=True)  8.95 us
    gather x5, local copies, waits for them, and re-layouts, arrange(): return jnp.take(shaped, order_index, axis=0).reshape(values.shape)  7.33 us
    all_to_all x1, starting transfers between devices, local(): lax.all_to_all(outbound[2], 'expert', split_axis=0, concat_axis=0, tiled=...  7.28 us
    all_to_all x1, starting transfers between devices, local(): lax.all_to_all(input_grad, 'expert', split_axis=0, concat_axis=0, tiled=T...  6 us
    select_n x5, other arithmetic, arrange(): return jnp.take(shaped, order_index, axis=0).reshape(values.shape)  4.18 us
  transfers between devices with their start and end apart: 6, of which 2 were waited for; matrix products, arithmetic and copies ran while one was open for 22% of the time, Pallas kernels for 0%

commit v1 on v0

--- a/solution.py
+++ b/solution.py
@@ -1,7 +1,38 @@
+import functools
 import jax
 import jax.numpy as jnp
 from jax import lax
 from jax.sharding import PartitionSpec as P
+
+
+def _show_sources_all(mat, out_dim, x_part):
+    state_next = mat.shape
+    d_next = mat.reshape(
+        *state_next[:out_dim], x_part, state_next[out_dim] // x_part, *state_next[out_dim + 1 :]
+    )
+    return jnp.moveaxis(d_next, out_dim, 0)
+
+
+def form_the_map(incoming_x, join_dim):
+    incoming_x = jnp.moveaxis(incoming_x, 0, join_dim)
+    reached = incoming_x.shape
+    return incoming_x.reshape(
+        *reached[:join_dim], reached[join_dim] * reached[join_dim + 1], *reached[join_dim + 2 :]
+    )
+
+
+def report_strips_all(view, mesh_ax, panel, target):
+    y2, s_next = (lax.axis_size(mesh_ax), lax.axis_index(mesh_ax))
+    n_now = _show_sources_all(view, target, y2)
+    by_rank = [n_now[s_next]]
+    for dev in range(1, y2):
+        o_now = n_now[s_next ^ dev]
+        by_rank.append(lax.ppermute(o_now, mesh_ax, [(c, c ^ dev) for c in range(y2)]))
+    n_now = jnp.stack(by_rank, axis=0)[s_next ^ jnp.arange(y2)]
+    return form_the_map(n_now, panel)
+
+
+steps_all_save = functools.partial(report_strips_all, mesh_ax="expert", panel=0, target=0)
 
 
 def silu_slope(pre_act):
@@ -55,7 +86,7 @@
         pre_grad, up_mat, contract_last, preferred_element_type=jnp.float32
     ).astype(jnp.bfloat16)
     returned, gate_back = (
-        lax.all_to_all(input_grad, "expert", split_axis=0, concat_axis=0, tiled=True),
+        steps_all_save(input_grad),
         lax.all_to_all(gate_grad, "expert", split_axis=0, concat_axis=0, tiled=True),
     )
     columns = (

time: 129 us -> 136 us (1.054)
  blocking collectives: 42.8 us -> 16.6 us
  waiting for transfers between devices: 14.8 us -> 29.8 us
  starting transfers between devices: 28.8 us -> 40.8 us
  local copies, waits for them, and re-layouts: 15.9 us -> 26.7 us
  matrix products: 16 us -> 13.2 us
  other arithmetic: 8.8 us -> 7.01 us
    all_to_all x1 -> x0, blocking collectives: 19.8 us -> none  [local(): lax.all_to_all(outbound[0], 'expert', split_axis=0, concat_axis=0, tiled=...]
    all_to_all x1, waiting for transfers between devices: 0.01 us -> 14 us  [local(): lax.all_to_all(outbound[0], 'expert', split_axis=0, concat_axis=0, tiled=...]
    ppermute x0 -> x7, starting transfers between devices: none -> 12.5 us  [report_strips_all(): lax.ppermute(o_now, mesh_ax, [(c, c ^ dev) for c in range(y2)])]
    unnamed x3 -> x15, local copies, waits for them, and re-layouts: 0.01 us -> 8.81 us
    all_gather x1, blocking collectives: 14 us -> 8.82 us  [local(): lax.all_gather(pre_grad, 'dp', axis=0, tiled=True)]
    all_to_all x1, waiting for transfers between devices: 0.01 us -> 4.83 us  [local(): lax.all_to_all(scaled, 'dp', split_axis=1, concat_axis=0, tiled=True)]
    all_to_all x1, waiting for transfers between devices: 3.64 us -> 0.01 us  [local(): lax.all_to_all(inputs, 'dp', split_axis=1, concat_axis=0, tiled=True)]
    gather x0 -> x1, local copies, waits for them, and re-layouts: none -> 2.41 us  [report_strips_all(): n_now = jnp.stack(by_rank, axis=0)[s_next ^ jnp.arange(y2)]]
  transfers between devices with their start and end apart: 6 -> 13, of which waited for: 2 -> 5; matrix products, arithmetic and copies ran while one was open for 22% -> 25% of each run, Pallas kernels for 0% -> 0%
where the time goes in v1:
time: 136 us; the launch traced here: 135 us
  starting transfers between devices  40.8 us (30%)
  waiting for transfers between devices  29.8 us (22%)
  local copies, waits for them, and re-layouts  26.7 us (20%)
  blocking collectives  16.6 us (12%)
  matrix products  13.2 us (10%)
  other arithmetic  7.01 us (5%)
    all_to_all x1, waiting for transfers between devices, local(): lax.all_to_all(outbound[0], 'expert', split_axis=0, concat_axis=0, tiled=...  14 us
    ppermute x7, starting transfers between devices, report_strips_all(): lax.ppermute(o_now, mesh_ax, [(c, c ^ dev) for c in range(y2)])  12.5 us
    all_to_all x1, waiting for transfers between devices, local(): lax.all_to_all(outbound[1], 'expert', split_axis=0, concat_axis=0, tiled=...  10.8 us
    all_gather x1, blocking collectives, local(): lax.all_gather(pre_grad, 'dp', axis=0, tiled=True)  8.82 us
    unnamed x15, local copies, waits for them, and re-layouts  8.81 us
    all_gather x1, blocking collectives, local(): lax.all_gather(hidden, 'dp', axis=0, tiled=True)  7.8 us
    all_to_all x1, starting transfers between devices, local(): lax.all_to_all(outbound[2], 'expert', split_axis=0, concat_axis=0, tiled=...  7.28 us
    gather x5, local copies, waits for them, and re-layouts, arrange(): return jnp.take(shaped, order_index, axis=0).reshape(values.shape)  6.79 us
  transfers between devices with their start and end apart: 13, of which 5 were waited for; matrix products, arithmetic and copies ran while one was open for 25% of the time, Pallas kernels for 0%

profile of v1, /device:TPU:0, one launch (start us, length us, event | category | flops | bytes accessed | tf_op | source)
XLA Modules:
  0.0 134.9 jit_solution(15091418735628732627)
XLA Ops:
  0.6 0.0 copy-start
  0.6 1.0 select_reduce_fusion.1
  1.7 0.1 select_reduce_fusion
  1.8 0.7 reshape.127
  2.5 0.6 gather_fusion.1
  3.1 0.1 select_bitcast_fusion
  3.2 0.6 copy.31
  3.8 7.3 %all-to-all-start = ((bf16[8,16,1]{1,2,0:T(2,128)(2,1)}), bf16[8,16,1]{1,2,0:T(2,128)(2,1)S(1)}, u32[]{:S(2)}, u32[]{:S(2)}) async-start(bf16[8,16,1]{1,2,0:T(2,128)(2,1)} %copy.31), calls=%async_computation | async-start | bytes 8192 | tf_op jit(solution)/shard_map/all_to_all | solution.py:69
  11.1 1.6 %gather_fusion.3 = bf16[8,16,2048]{2,1,0:T(8,128)(2,1)S(1)} fusion(bf16[8,16,2048]{2,1,0:T(8,128)(2,1)} %bitcast.98, s32[1024]{0:T(1024)S(1)} %pad_clamp_fusion.2), kind=kCustom, calls=%fused_computation.3.clone | custom fusion | bytes 1048608 | tf_op jit(solution)/shard_map/jit(_take)/gather | solution.py:45
  12.7 2.4 %gather_fusion.2 = bf16[8,16,2048]{2,1,0:T(8,128)(2,1)} fusion(bf16[8,16,2048]{2,1,0:T(8,128)(2,1)} %bitcast.99, s32[1024]{0:T(1024)S(1)} %pad_clamp_fusion.2), kind=kCustom, calls=%fused_computation.1.clone | custom fusion | bytes 1048608 | tf_op jit(solution)/shard_map/jit(_take)/gather | solution.py:45
  15.1 2.2 %broadcast_select_fusion.1 = (bf16[8,16,2048]{2,1,0:T(8,128)(2,1)}, bf16[8,16,2048]{2,1,0:T(8,128)(2,1)}) fusion(bf16[8,16,2048]{2,1,0:T(8,128)(2,1)S(1)} %gather_fusion.3, pred[8]{0:T(512)(128)(4,1)S(1)} %compare_and_fusion.1, bf16[8,16,2048]{2,1,0:T(8,128)(2,1)} %gather_fusion.2), kind=kLoop, calls=%fused_computation.31 | loop fusion | flops 524288 | bytes 2097160 | tf_op jit(solution)/shard_map/jit(_take)/select_n | solution.py:45
  17.3 0.2 all-to-all-done
  17.5 5.8 %all-to-all-start.2 = ((bf16[8,16,2048]{2,1,0:T(8,128)(2,1)}), bf16[8,16,2048]{2,1,0:T(8,128)(2,1)S(1)}, u32[]{:S(2)}, u32[]{:S(2)}) async-start(bf16[8,16,2048]{2,1,0:T(8,128)(2,1)} %get-tuple-element.16), calls=%async_computation.2 | async-start | bytes 1048576 | tf_op jit(solution)/shard_map/all_to_all | solution.py:67
  23.3 14.0 %all-to-all-done.2 = bf16[8,16,2048]{2,1,0:T(8,128)(2,1)S(1)} async-done(((bf16[8,16,2048]{2,1,0:T(8,128)(2,1)}), bf16[8,16,2048]{2,1,0:T(8,128)(2,1)S(1)}, u32[]{:S(2)}, u32[]{:S(2)}) %all-to-all-start.2) | async-done | bytes 524320 | tf_op jit(solution)/shard_map/all_to_all | solution.py:67
  37.2 0.8 copy-done.2
  38.0 3.6 %all-to-all-start.1 = ((bf16[8,16,2048]{2,1,0:T(8,128)(2,1)}), bf16[8,16,2048]{2,1,0:T(8,128)(2,1)S(1)}, u32[]{:S(2)}, u32[]{:S(2)}) async-start(bf16[8,16,2048]{2,1,0:T(8,128)(2,1)} %get-tuple-element.17), calls=%async_computation.1 | async-start | bytes 1048576 | tf_op jit(solution)/shard_map/all_to_all | solution.py:68
  41.8 0.6 reshape.138
  42.4 2.8 %multiply_convert_fusion.1 = (bf16[128,704]{0,1:T(8,128)(2,1)}, f32[128,704]{0,1:T(8,128)}) fusion(bf16[128,2048]{1,0:T(8,128)(2,1)} %bitcast.96, bf16[1,2048,704]{1,2,0:T(8,128)(2,1)S(1)} %copy-done), kind=kOutput, calls=%fused_computation.33 | convolution fusion | flops 369549312 | bytes 3948544 | tf_op jit(solution)/shard_map/dot_general | solution.py:74
  45.1 10.8 %all-to-all-done.1 = bf16[8,16,2048]{2,1,0:T(8,128)(2,1)S(1)} async-done(((bf16[8,16,2048]{2,1,0:T(8,128)(2,1)}), bf16[8,16,2048]{2,1,0:T(8,128)(2,1)S(1)}, u32[]{:S(2)}, u32[]{:S(2)}) %all-to-all-start.1) | async-done | bytes 524320 | tf_op jit(solution)/shard_map/all_to_all | solution.py:68
  55.9 0.2 multiply_convert_fusion
  56.1 2.8 %fusion.20 = bf16[128,704]{0,1:T(8,128)(2,1)S(1)} fusion(bf16[128,2048]{1,0:T(8,128)(2,1)S(1)} %bitcast.97, bf16[1,2048,704]{1,2,0:T(8,128)(2,1)} %param.17, f32[128,704]{0,1:T(8,128)} %get-tuple-element.19), kind=kOutput, calls=%fused_computation.20 | convolution fusion | flops 369909760 | bytes 3948544 | tf_op jit(solution)/shard_map/dot_general | solution.py:83
  58.8 0.6 fusion.11
  59.5 0.0 copy-start.1
  59.5 8.8 %all_gather.6 = bf16[512,704]{0,1:T(8,128)(2,1)} all-gather(bf16[128,704]{0,1:T(8,128)(2,1)S(1)} %fusion.20), channel_id=1, replica_groups=mesh['dp'=4,'expert'=8] {'dp'}, dimensions={0}, use_global_device_ids=true | all-gather | bytes 901120 | tf_op jit(solution)/shard_map/all_gather | solution.py:97
  68.3 0.7 dynamic-slice_bitcast_fusion
  69.0 1.4 %collective-permute-start = (bf16[16,2048]{1,0:T(8,128)(2,1)}, bf16[16,2048]{1,0:T(8,128)(2,1)}, u32[]{:S(2)}, u32[]{:S(2)}) collective-permute-start(bf16[16,2048]{1,0:T(8,128)(2,1)} %get-tuple-element.12), channel_id=1, source_target_pairs={{0,1},{1,0},{2,3},{3,2},{4,5},{5,4},{6,7},{7,6},{8,9},{9,8},{10,11... | collective-permute-start | bytes 196616 | tf_op jit(solution)/shard_map/ppermute | solution.py:30
  70.5 0.0 collective-permute-start.1
  70.5 2.1 %collective-permute-start.2 = (bf16[16,2048]{1,0:T(8,128)(2,1)}, bf16[16,2048]{1,0:T(8,128)(2,1)}, u32[]{:S(2)}, u32[]{:S(2)}) collective-permute-start(bf16[16,2048]{1,0:T(8,128)(2,1)} %get-tuple-element.10), channel_id=1, source_target_pairs={{0,3},{1,2},{2,1},{3,0},{4,7},{5,6},{6,5},{7,4},{8,11},{9,10},{10,... | collective-permute-start | bytes 196616 | tf_op jit(solution)/shard_map/ppermute | solution.py:30
  72.5 0.4 collective-permute-start.3
  72.9 3.4 %collective-permute-start.4 = (bf16[16,2048]{1,0:T(8,128)(2,1)}, bf16[16,2048]{1,0:T(8,128)(2,1)}, u32[]{:S(2)}, u32[]{:S(2)}) collective-permute-start(bf16[16,2048]{1,0:T(8,128)(2,1)} %get-tuple-element.8), channel_id=1, source_target_pairs={{0,5},{1,4},{2,7},{3,6},{4,1},{5,0},{6,3},{7,2},{8,13},{9,12},{10,... | collective-permute-start | bytes 196616 | tf_op jit(solution)/shard_map/ppermute | solution.py:30
  76.3 7.8 %all_gather.7 = bf16[512,704]{0,1:T(8,128)(2,1)} all-gather(bf16[128,704]{0,1:T(8,128)(2,1)S(1)} %copy-done.3), channel_id=1, replica_groups=mesh['dp'=4,'expert'=8] {'dp'}, dimensions={0}, use_global_device_ids=true | all-gather | bytes 901120 | tf_op jit(solution)/shard_map/all_gather | solution.py:98
  84.1 0.1 convert_element_type.77
  84.2 0.7 fusion.14
  84.9 0.7 convert_element_type.98
  85.6 3.3 %all-to-all-start.3 = ((bf16[8,16,1]{1,2,0:T(2,128)(2,1)}), bf16[8,16,1]{1,2,0:T(2,128)(2,1)S(1)}, u32[]{:S(2)}, u32[]{:S(2)}) async-start(bf16[8,16,1]{1,2,0:T(2,128)(2,1)} %convert_element_type.98), calls=%async_computation.3 | async-start | bytes 8192 | tf_op jit(solution)/shard_map/all_to_all | solution.py:90
  88.9 1.7 %reshape.139 = f32[128,4,512]{2,1,0:T(4,128)} reshape(bf16[8,16,2048]{2,1,0:T(8,128)(2,1)S(1)} %all-to-all-done.1) | data formatting | bytes 1572864 | tf_op jit(solution)/shard_map/convert_element_type | solution.py:80
  90.6 2.4 %fusion.23 = bf16[128,4,512]{2,0,1:T(8,128)(2,1)} fusion(f32[128,4,512]{2,1,0:T(4,128)} %reshape.139, f32[128]{0:T(128)} %reshape.138), kind=kLoop, calls=%fused_computation.22 | loop fusion | flops 524288 | bytes 1573376 | tf_op jit(solution)/shard_map/convert_element_type | solution.py:80
  93.0 1.4 %all_to_all.48 = bf16[128,4,512]{2,1,0:T(4,128)(2,1)S(1)} reshape(bf16[8,16,2048]{2,1,0:T(8,128)(2,1)} %copy-done.2) | data formatting | bytes 1048576 | tf_op jit(solution)/shard_map/all_to_all | solution.py:93
  94.4 0.9 copy.34
  95.3 0.1 all-to-all-done.3
  95.3 4.1 %all-to-all-start.4 = ((bf16[128,4,512]{2,0,1:T(8,128)(2,1)}), bf16[128,4,512]{2,0,1:T(8,128)(2,1)}, u32[]{:S(2)}, u32[]{:S(2)}) async-start(bf16[128,4,512]{2,0,1:T(8,128)(2,1)} %copy.34), calls=%async_computation.4 | async-start | bytes 1048576 | tf_op jit(solution)/shard_map/all_to_all | solution.py:93
  99.5 0.6 gather_fusion.5
  100.1 0.1 broadcast_select_fusion.3
  100.1 0.6 reshape.133
  100.7 0.0 collective-permute-done
  100.7 3.8 %collective-permute-start.5 = (bf16[16,2048]{1,0:T(8,128)(2,1)S(1)}, bf16[16,2048]{1,0:T(8,128)(2,1)S(1)}, u32[]{:S(2)}, u32[]{:S(2)}) collective-permute-start(bf16[16,2048]{1,0:T(8,128)(2,1)S(1)} %get-tuple-element.7), channel_id=1, source_target_pairs={{0,6},{1,7},{2,4},{3,5},{4,2},{5,3},{6,0},{7,1},{8,14},{9,15},{10,... | collective-permute-start | bytes 196616 | tf_op jit(solution)/shard_map/ppermute | solution.py:30
  104.5 1.5 %bitcast_dynamic-update-slice_fusion.6 = bf16[8,16,2048]{2,1,0:T(8,128)(2,1)} fusion(bf16[8,16,2048]{2,1,0:T(8,128)(2,1)} %get-tuple-element.13, bf16[16,2048]{1,0:T(8,128)(2,1)} %collective-permute-done), kind=kLoop, calls=%fused_computation.41 | loop fusion | bytes 131072
  106.0 0.0 collective-permute-done.1
  106.0 1.5 %collective-permute-start.6 = (bf16[16,2048]{1,0:T(8,128)(2,1)S(1)}, bf16[16,2048]{1,0:T(8,128)(2,1)S(1)}, u32[]{:S(2)}, u32[]{:S(2)}) collective-permute-start(bf16[16,2048]{1,0:T(8,128)(2,1)S(1)} %get-tuple-element.6), channel_id=1, source_target_pairs={{0,7},{1,6},{2,5},{3,4},{4,3},{5,2},{6,1},{7,0},{8,15},{9,14},{10,... | collective-permute-start | bytes 196616 | tf_op jit(solution)/shard_map/ppermute | solution.py:30
  107.5 1.5 %bitcast_dynamic-update-slice_fusion.5 = bf16[8,16,2048]{2,1,0:T(8,128)(2,1)} fusion(bf16[8,16,2048]{2,1,0:T(8,128)(2,1)} %bitcast_dynamic-update-slice_fusion.6, bf16[16,2048]{1,0:T(8,128)(2,1)} %collective-permute-done.1), kind=kLoop, calls=%fused_computation.40 | loop fusion | bytes 131072
  108.9 1.5 %bitcast_dynamic-update-slice_fusion.4 = bf16[8,16,2048]{2,1,0:T(8,128)(2,1)} fusion(bf16[8,16,2048]{2,1,0:T(8,128)(2,1)} %bitcast_dynamic-update-slice_fusion.5, bf16[16,2048]{1,0:T(8,128)(2,1)} %collective-permute-done.2), kind=kLoop, calls=%fused_computation.39 | loop fusion | bytes 131072
  110.4 1.5 %bitcast_dynamic-update-slice_fusion.3 = bf16[8,16,2048]{2,1,0:T(8,128)(2,1)} fusion(bf16[8,16,2048]{2,1,0:T(8,128)(2,1)} %bitcast_dynamic-update-slice_fusion.4, bf16[16,2048]{1,0:T(8,128)(2,1)} %collective-permute-done.3), kind=kLoop, calls=%fused_computation.38 | loop fusion | bytes 131072
  111.9 1.5 %bitcast_dynamic-update-slice_fusion.2 = bf16[8,16,2048]{2,1,0:T(8,128)(2,1)} fusion(bf16[8,16,2048]{2,1,0:T(8,128)(2,1)} %bitcast_dynamic-update-slice_fusion.3, bf16[16,2048]{1,0:T(8,128)(2,1)} %collective-permute-done.4), kind=kLoop, calls=%fused_computation.37 | loop fusion | bytes 131072
  113.4 0.0 collective-permute-done.5
  113.4 0.6 bitcast_dynamic-update-slice_fusion.1
  114.0 0.0 collective-permute-done.6
  114.0 0.6 bitcast_dynamic-update-slice_fusion
  114.6 2.4 %gather_fusion = bf16[8,16,2048]{2,1,0:T(8,128)(2,1)} fusion(bf16[8,16,2048]{2,1,0:T(8,128)(2,1)} %bitcast_dynamic-update-slice_fusion, s32[1024]{0:T(1024)S(1)} %pad_clamp_fusion.1), kind=kCustom, calls=%fused_computation.5 | custom fusion | bytes 1048608 | tf_op jit(solution)/shard_map/gather | solution.py:31
  117.0 1.6 %gather_fusion.4 = bf16[8,16,2048]{2,1,0:T(8,128)(2,1)S(1)} fusion(bf16[8,16,2048]{2,1,0:T(8,128)(2,1)} %gather_fusion, s32[1024]{0:T(1024)S(1)} %pad_clamp_fusion), kind=kCustom, calls=%fused_computation.4.clone | custom fusion | bytes 1048608 | tf_op jit(solution)/shard_map/jit(_take)/gather | solution.py:45
  118.7 4.2 %all-to-all-start.5 = ((bf16[128,4,512]{2,0,1:T(8,128)(2,1)}), bf16[128,4,512]{2,0,1:T(8,128)(2,1)}, u32[]{:S(2)}, u32[]{:S(2)}) async-start(bf16[128,4,512]{2,0,1:T(8,128)(2,1)} %fusion.23), calls=%async_computation.5 | async-start | bytes 1048576 | tf_op jit(solution)/shard_map/all_to_all | solution.py:94
  122.8 0.9 broadcast_select_fusion
  123.7 3.2 %convert_reduce_fusion.1 = bf16[512,704]{0,1:T(8,128)(2,1)} fusion(bf16[128,4,512]{2,0,1:T(8,128)(2,1)} %all-to-all-done.4, bf16[512,704]{0,1:T(8,128)(2,1)} %all_gather.6), kind=kOutput, calls=%fused_computation.15 | convolution fusion | flops 371621888 | bytes 1966080 | tf_op jit(solution)/shard_map/krc,krh->kch/dot_general | solution.py:106
  126.9 4.8 %all-to-all-done.5 = bf16[128,4,512]{2,0,1:T(8,128)(2,1)} async-done(((bf16[128,4,512]{2,0,1:T(8,128)(2,1)}), bf16[128,4,512]{2,0,1:T(8,128)(2,1)}, u32[]{:S(2)}, u32[]{:S(2)}) %all-to-all-start.5) | async-done | bytes 524320 | tf_op jit(solution)/shard_map/all_to_all | solution.py:94
  131.7 3.2 %convert_reduce_fusion = bf16[512,704]{0,1:T(8,128)(2,1)} fusion(bf16[128,4,512]{2,0,1:T(8,128)(2,1)} %all-to-all-done.5, bf16[512,704]{0,1:T(8,128)(2,1)} %all_gather.7), kind=kOutput, calls=%fused_computation.14 | convolution fusion | flops 371621888 | bytes 1966080 | tf_op jit(solution)/shard_map/krc,krh->kch/dot_general | solution.py:109
  (19 shorter events, 0.1 us)
Async XLA Ops:
  0.6 41.7 %copy-start = (bf16[1,2048,704]{1,2,0:T(8,128)(2,1)S(1)}, bf16[1,2048,704]{1,2,0:T(8,128)(2,1)}, u32[]{:S(2)}) copy-start(bf16[1,2048,704]{1,2,0:T(8,128)(2,1)} %param.16) | copy-start | bytes 8650756
  3.8 13.7 %all-to-all-start = ((bf16[8,16,1]{1,2,0:T(2,128)(2,1)}), bf16[8,16,1]{1,2,0:T(2,128)(2,1)S(1)}, u32[]{:S(2)}, u32[]{:S(2)}) async-start(bf16[8,16,1]{1,2,0:T(2,128)(2,1)} %copy.31), calls=%async_computation | async-start | bytes 8192 | tf_op jit(solution)/shard_map/all_to_all | solution.py:69
  17.5 19.8 %all-to-all-start.2 = ((bf16[8,16,2048]{2,1,0:T(8,128)(2,1)}), bf16[8,16,2048]{2,1,0:T(8,128)(2,1)S(1)}, u32[]{:S(2)}, u32[]{:S(2)}) async-start(bf16[8,16,2048]{2,1,0:T(8,128)(2,1)} %get-tuple-element.16), calls=%async_computation.2 | async-start | bytes 1048576 | tf_op jit(solution)/shard_map/all_to_all | solution.py:67
  37.2 0.8 copy-start.2
  38.0 17.9 %all-to-all-start.1 = ((bf16[8,16,2048]{2,1,0:T(8,128)(2,1)}), bf16[8,16,2048]{2,1,0:T(8,128)(2,1)S(1)}, u32[]{:S(2)}, u32[]{:S(2)}) async-start(bf16[8,16,2048]{2,1,0:T(8,128)(2,1)} %get-tuple-element.17), calls=%async_computation.1 | async-start | bytes 1048576 | tf_op jit(solution)/shard_map/all_to_all | solution.py:68
  58.8 17.5 %copy-start.3 = (bf16[128,704]{0,1:T(8,128)(2,1)S(1)}, bf16[128,704]{0,1:T(8,128)(2,1)}, u32[]{:S(2)}) copy-start(bf16[128,704]{0,1:T(8,128)(2,1)} %get-tuple-element.18) | copy-start | bytes 540676
  59.5 24.8 %copy-start.1 = (bf16[1,2048,704]{1,2,0:T(8,128)(2,1)S(1)}, bf16[1,2048,704]{1,2,0:T(8,128)(2,1)}, u32[]{:S(2)}) copy-start(bf16[1,2048,704]{1,2,0:T(8,128)(2,1)} %param.17) | copy-start | bytes 8650756
  69.0 31.7 %collective-permute-start = (bf16[16,2048]{1,0:T(8,128)(2,1)}, bf16[16,2048]{1,0:T(8,128)(2,1)}, u32[]{:S(2)}, u32[]{:S(2)}) collective-permute-start(bf16[16,2048]{1,0:T(8,128)(2,1)} %get-tuple-element.12), channel_id=1, source_target_pairs={{0,1},{1,0},{2,3},{3,2},{4,5},{5,4},{6,7},{7,6},{8,9},{9,8},{10,11... | collective-permute-start | bytes 196616 | tf_op jit(solution)/shard_map/ppermute | solution.py:30
  70.5 35.5 %collective-permute-start.1 = (bf16[16,2048]{1,0:T(8,128)(2,1)}, bf16[16,2048]{1,0:T(8,128)(2,1)}, u32[]{:S(2)}, u32[]{:S(2)}) collective-permute-start(bf16[16,2048]{1,0:T(8,128)(2,1)} %get-tuple-element.11), channel_id=1, source_target_pairs={{0,2},{1,3},{2,0},{3,1},{4,6},{5,7},{6,4},{7,5},{8,10},{9,11},{10,... | collective-permute-start | bytes 196616 | tf_op jit(solution)/shard_map/ppermute | solution.py:30
  70.5 38.5 %collective-permute-start.2 = (bf16[16,2048]{1,0:T(8,128)(2,1)}, bf16[16,2048]{1,0:T(8,128)(2,1)}, u32[]{:S(2)}, u32[]{:S(2)}) collective-permute-start(bf16[16,2048]{1,0:T(8,128)(2,1)} %get-tuple-element.10), channel_id=1, source_target_pairs={{0,3},{1,2},{2,1},{3,0},{4,7},{5,6},{6,5},{7,4},{8,11},{9,10},{10,... | collective-permute-start | bytes 196616 | tf_op jit(solution)/shard_map/ppermute | solution.py:30
  72.5 37.9 %collective-permute-start.3 = (bf16[16,2048]{1,0:T(8,128)(2,1)}, bf16[16,2048]{1,0:T(8,128)(2,1)}, u32[]{:S(2)}, u32[]{:S(2)}) collective-permute-start(bf16[16,2048]{1,0:T(8,128)(2,1)} %get-tuple-element.9), channel_id=1, source_target_pairs={{0,4},{1,5},{2,6},{3,7},{4,0},{5,1},{6,2},{7,3},{8,12},{9,13},{10,... | collective-permute-start | bytes 196616 | tf_op jit(solution)/shard_map/ppermute | solution.py:30
  72.9 39.0 %collective-permute-start.4 = (bf16[16,2048]{1,0:T(8,128)(2,1)}, bf16[16,2048]{1,0:T(8,128)(2,1)}, u32[]{:S(2)}, u32[]{:S(2)}) collective-permute-start(bf16[16,2048]{1,0:T(8,128)(2,1)} %get-tuple-element.8), channel_id=1, source_target_pairs={{0,5},{1,4},{2,7},{3,6},{4,1},{5,0},{6,3},{7,2},{8,13},{9,12},{10,... | collective-permute-start | bytes 196616 | tf_op jit(solution)/shard_map/ppermute | solution.py:30
  85.6 9.7 %all-to-all-start.3 = ((bf16[8,16,1]{1,2,0:T(2,128)(2,1)}), bf16[8,16,1]{1,2,0:T(2,128)(2,1)S(1)}, u32[]{:S(2)}, u32[]{:S(2)}) async-start(bf16[8,16,1]{1,2,0:T(2,128)(2,1)} %convert_element_type.98), calls=%async_computation.3 | async-start | bytes 8192 | tf_op jit(solution)/shard_map/all_to_all | solution.py:90
  95.3 23.3 %all-to-all-start.4 = ((bf16[128,4,512]{2,0,1:T(8,128)(2,1)}), bf16[128,4,512]{2,0,1:T(8,128)(2,1)}, u32[]{:S(2)}, u32[]{:S(2)}) async-start(bf16[128,4,512]{2,0,1:T(8,128)(2,1)} %copy.34), calls=%async_computation.4 | async-start | bytes 1048576 | tf_op jit(solution)/shard_map/all_to_all | solution.py:93
  100.7 12.6 %collective-permute-start.5 = (bf16[16,2048]{1,0:T(8,128)(2,1)S(1)}, bf16[16,2048]{1,0:T(8,128)(2,1)S(1)}, u32[]{:S(2)}, u32[]{:S(2)}) collective-permute-start(bf16[16,2048]{1,0:T(8,128)(2,1)S(1)} %get-tuple-element.7), channel_id=1, source_target_pairs={{0,6},{1,7},{2,4},{3,5},{4,2},{5,3},{6,0},{7,1},{8,14},{9,15},{10,... | collective-permute-start | bytes 196616 | tf_op jit(solution)/shard_map/ppermute | solution.py:30
  106.0 8.0 %collective-permute-start.6 = (bf16[16,2048]{1,0:T(8,128)(2,1)S(1)}, bf16[16,2048]{1,0:T(8,128)(2,1)S(1)}, u32[]{:S(2)}, u32[]{:S(2)}) collective-permute-start(bf16[16,2048]{1,0:T(8,128)(2,1)S(1)} %get-tuple-element.6), channel_id=1, source_target_pairs={{0,7},{1,6},{2,5},{3,4},{4,3},{5,2},{6,1},{7,0},{8,15},{9,14},{10,... | collective-permute-start | bytes 196616 | tf_op jit(solution)/shard_map/ppermute | solution.py:30
  118.7 13.1 %all-to-all-start.5 = ((bf16[128,4,512]{2,0,1:T(8,128)(2,1)}), bf16[128,4,512]{2,0,1:T(8,128)(2,1)}, u32[]{:S(2)}, u32[]{:S(2)}) async-start(bf16[128,4,512]{2,0,1:T(8,128)(2,1)} %fusion.23), calls=%async_computation.5 | async-start | bytes 1048576 | tf_op jit(solution)/shard_map/all_to_all | solution.py:94
